TPU v7x, 32 devices: a whole 2x2x4 slice. The times are simulated.
32 devices in a mesh: groups: 2 (over y), frame: 8 (over z, x), row: 2 (over core).
Axes of the slice: x: 2, y: 2, z: 4, core: 2. Of those that a mesh axis runs over, the one named last changes fastest.
Arguments:
- latent: bfloat16 [16, 16, 64, 640], P(('groups', 'frame'), 'row'), parts along dimension 0, may hold values from -18 to 18
- norm_gain: float32 [640], replicated, may hold values from 0.1 to 1.9
- time_kernel: bfloat16 [3, 640, 640], replicated, may hold values from -0.125 to 0.125
- space_norm: float32 [640], replicated, may hold values from 0.1 to 1.9
- space_qkv: bfloat16 [640, 1920], replicated, may hold values from -12 to 12
- space_out: bfloat16 [640, 640], replicated, may hold values from -0.25 to 0.25
- time_norm: float32 [640], replicated, may hold values from 0.1 to 1.9
- time_qkv: bfloat16 [640, 1920], replicated, may hold values from -12 to 12
- time_out: bfloat16 [640, 640], replicated, may hold values from -0.25 to 0.25
Outputs:
- output: float32 [16, 16, 64, 640], P(('groups', 'frame'), 'row'), parts along dimension 0
There are 2 independent parts, one for each index of `groups`. A program takes and returns all parts, laid end to end along the dimension named above; an argument that names none is the same for every part. Nothing has to cross between parts.
All inputs are finite; a program needn't handle non-finite values.
Results may differ from a plain program's by a relative error of at most 0.0018.
Values may be sent and summed in bfloat16 or wider, within the bound.
A program may use at most 128 MiB of HBM per device.

v0:
```python
import jax
import jax.numpy as jnp
from jax import lax
from jax.sharding import PartitionSpec as P

HEADS = 10
GROUPS = 32
epsilon = 1e-05


def padded_2(block, sides, width):
    for axis, dim in sides:
        count = lax.axis_size(axis)
        forward = [(i, i + 1) for i in range(count - 1)]
        backward = [(target, source) for source, target in forward]
        low = lax.ppermute(
            lax.slice_in_dim(block, block.shape[dim] - width, None, axis=dim), axis, forward
        )
        high = lax.ppermute(lax.slice_in_dim(block, 0, width, axis=dim), axis, backward)
        block = jnp.concatenate([low, block, high], axis=dim)
    return block


def normalize_silu(grouped, first, second, number, gain, shape):
    center = first / number
    spread = second / number - center * center
    scaling = lax.rsqrt(spread + epsilon)
    normed = ((grouped - center[:, None]) * scaling[:, None]).reshape(shape) * gain
    return jax.nn.silu(normed).astype(jnp.bfloat16)


def layer_norm(inputs, gain):
    center = jnp.mean(inputs, axis=-1, keepdims=True)
    shifted = inputs - center
    spread = jnp.mean(shifted * shifted, axis=-1, keepdims=True)
    return (shifted * lax.rsqrt(spread + epsilon) * gain).astype(jnp.bfloat16)


def project_three(inputs, weight):
    channels = weight.shape[0]
    lead = inputs.shape[:-1]
    packed = jnp.dot(
        inputs.reshape(-1, channels), weight, preferred_element_type=jnp.float32
    ).astype(jnp.bfloat16)
    packed = packed.reshape(lead + (3 * channels,))
    return (
        packed[..., :channels],
        packed[..., channels : 2 * channels],
        packed[..., 2 * channels :],
    )


def time_attend(queries, key_rows, values):
    frames, pixels, channels = queries.shape
    head_size = channels // HEADS
    query_heads = queries.reshape(frames, pixels, HEADS, head_size)
    key_heads = key_rows.reshape(frames, pixels, HEADS, head_size)
    value_heads = values.reshape(frames, pixels, HEADS, head_size)
    scores = jnp.einsum(
        "qphd,kphd->phqk", query_heads, key_heads, preferred_element_type=jnp.float32
    ) * head_size ** (-0.5)
    raised = jnp.exp(scores - jnp.max(scores, axis=-1, keepdims=True))
    weight_sum = jnp.sum(raised, axis=-1)
    weights = raised.astype(jnp.bfloat16)
    result = jnp.einsum("phqk,kphd->qphd", weights, value_heads, preferred_element_type=jnp.float32)
    result = result / jnp.transpose(weight_sum, (2, 0, 1))[:, :, :, None]
    return result.astype(jnp.bfloat16).reshape(frames, pixels, channels)


def add_projected(base, attended, weight):
    channels = weight.shape[0]
    summed = base.reshape(-1, channels) + jnp.dot(
        attended.reshape(-1, channels), weight, preferred_element_type=jnp.float32
    )
    return summed.reshape(base.shape)


def body(
    latent, norm_gain, time_kernel, space_norm, space_qkv, space_out, time_norm, time_qkv, time_out
):
    frames, row_count, col_count, channels = latent.shape
    pixels = row_count * col_count
    per_group = channels // GROUPS
    head_size = channels // HEADS
    grouped = latent.astype(jnp.float32).reshape(frames, row_count, col_count, GROUPS, per_group)
    first = jnp.sum(grouped, axis=(0, 1, 2, 4))
    second = jnp.sum(grouped * grouped, axis=(0, 1, 2, 4))
    first, second = lax.psum((first, second), ("frame", "row"))
    number = frames * lax.axis_size("frame") * pixels * lax.axis_size("row") * per_group
    wide = padded_2(latent, (("frame", 0),), 1)
    wide_frames = wide.shape[0]
    wide_grouped = wide.astype(jnp.float32).reshape(
        wide_frames, row_count, col_count, GROUPS, per_group
    )
    padded = normalize_silu(wide_grouped, first, second, number, norm_gain, wide.shape)
    me, count = (lax.axis_index("frame"), lax.axis_size("frame"))
    place = me * frames - 1 + jnp.arange(wide_frames)
    inside = (place >= 0) & (place < count * frames)
    padded = jnp.where(inside[:, None, None, None], padded, jnp.zeros((), padded.dtype))
    mixed = jnp.zeros((frames * pixels, channels), jnp.float32)
    for tap in range(3):
        window = padded[tap : tap + frames].reshape(-1, channels)
        mixed = mixed + jnp.dot(window, time_kernel[tap], preferred_element_type=jnp.float32)
    stepped = latent.astype(jnp.float32).reshape(-1, channels) + mixed
    stepped = stepped.reshape(frames, pixels, channels)
    tokens = layer_norm(stepped, space_norm)
    queries, key_rows, values = project_three(tokens, space_qkv)
    query_heads = queries.reshape(frames, pixels, HEADS, head_size)
    top_score = jnp.full((frames, HEADS, pixels), -jnp.inf, jnp.float32)
    weight_sum = jnp.zeros((frames, HEADS, pixels), jnp.float32)
    partial_sum = jnp.zeros((frames, HEADS, pixels, head_size), jnp.float32)
    key_piece = lax.all_gather(key_rows, "row", axis=1, tiled=True)
    value_piece = lax.all_gather(values, "row", axis=1, tiled=True)
    key_count = key_piece.shape[1]
    key_heads = key_piece.reshape(frames, key_count, HEADS, head_size)
    value_heads = value_piece.reshape(frames, key_count, HEADS, head_size)
    scores = jnp.einsum(
        "fqhd,fkhd->fhqk", query_heads, key_heads, preferred_element_type=jnp.float32
    ) * head_size ** (-0.5)
    new_top = jnp.max(scores, axis=-1)
    rescale = jnp.exp(top_score - new_top)
    raised = jnp.exp(scores - new_top[..., None])
    weight_sum = weight_sum * rescale + jnp.sum(raised, axis=-1)
    weights = raised.astype(jnp.bfloat16)
    partial_sum = partial_sum * rescale[..., None] + jnp.einsum(
        "fhqk,fkhd->fhqd", weights, value_heads, preferred_element_type=jnp.float32
    )
    top_score, weight_sum, partial_sum = (new_top, weight_sum, partial_sum)
    attended = (partial_sum / weight_sum[..., None]).astype(jnp.bfloat16)
    attended = jnp.transpose(attended, (0, 2, 1, 3)).reshape(frames, pixels, channels)
    spaced = add_projected(stepped, attended, space_out)
    normed = layer_norm(spaced, time_norm)
    moved = lax.all_to_all(normed, "frame", split_axis=1, concat_axis=0, tiled=True)
    queries, key_rows, values = project_three(moved, time_qkv)
    result = time_attend(queries, key_rows, values)
    result = lax.all_to_all(result, "frame", split_axis=0, concat_axis=1, tiled=True)
    output = add_projected(spaced, result, time_out)
    return output.reshape(frames, row_count, col_count, channels)


def solution(mesh):
    return jax.shard_map(
        body,
        mesh=mesh,
        in_specs=(
            P(("groups", "frame"), "row", None, None),
            P(),
            P(),
            P(),
            P(),
            P(),
            P(),
            P(),
            P(),
        ),
        out_specs=P(("groups", "frame"), "row", None, None),
        check_vma=False,
    )
```

profile of v0, /device:TPU:0, one launch (start us, length us, event | category | flops | bytes accessed | tf_op | source)
XLA Modules:
  0.0 192.2 jit_solution(7589339824454949340)
XLA Ops:
  6.5 5.0 %collective-permute-start = (bf16[1,8,64,640]{3,2,1,0:T(8,128)(2,1)}, bf16[1,8,64,640]{3,2,1,0:T(8,128)(2,1)S(1)}, u32[]{:S(2)}, u32[]{:S(2)}) collective-permute-start(bf16[1,8,64,640]{3,2,1,0:T(8,128)(2,1)} %param.9), channel_id=1, source_target_pairs={{0,2},{2,4},{4,6},{6,8},{8,10},{10,12},{12,14},{1,3},{3,5},{5,7},{... | collective-permute-start | bytes 1966088 | tf_op jit(solution)/shard_map/ppermute | solution.py:16
  14.6 49.5 %all-reduce = (f32[32]{0:T(128)S(1)}, f32[32]{0:T(128)S(1)}) all-reduce(f32[32]{0:T(128)S(1)} %reduce_sum.91, f32[32]{0:T(128)S(1)} %reduce_sum.88), channel_id=1, replica_groups=mesh['groups'=2,'frame'=8,'row'=2] {'frame','row'}, use_global_device_ids=true, to_apply=%region_5.6 | all-reduce | flops 64 | bytes 512 | tf_op jit(solution)/shard_map/psum | solution.py:88
  64.5 2.5 %fusion.8 = bf16[3,8,64,640]{3,2,1,0:T(8,128)(2,1)S(1)} fusion(bf16[1,8,64,640]{3,2,1,0:T(8,128)(2,1)} %collective-permute-done.1, bf16[1,8,64,640]{3,2,1,0:T(8,128)(2,1)} %param.9, bf16[1,8,64,640]{3,2,1,0:T(8,128)(2,1)S(1)} %collective-permute-done, f32[640]{0:T(1024)} %param.10, f32[640]{0:T(1024)S(1)} %mul.99, f32[640]{0:T(1024)S(1)} %sub.69, ...), kind=kLoop, calls=%fused_computation.15 | loop fusion | flops 11796480 | bytes 3939843 | tf_op jit(solution)/shard_map/jit(_where)/select_n | solution.py:99
  71.9 1.9 fusion.4
  75.8 6.1 %all-gather.3.cloned.1.call-done = bf16[1,1024,640]{2,1,0:T(8,128)(2,1)} async-done(((bf16[1,512,640]{2,1,0:T(8,128)(2,1)}), bf16[1,1024,640]{2,1,0:T(8,128)(2,1)}) %all-gather.3.cloned.1.call-update) | async-done | bytes 1310736 | tf_op jit(solution)/shard_map/all_gather | solution.py:112
  81.9 1.6 copy.51
  83.5 3.0 %multiply_reduce_fusion = (f32[10,512]{1,0:T(8,128)S(1)}, f32[10,512,1024]{2,1,0:T(8,128)S(1)}) fusion(bf16[512,10,64]{0,2,1:T(8,128)(2,1)S(1)} %bitcast.69, bf16[1024,10,64]{0,2,1:T(8,128)(2,1)S(1)} %bitcast.63), kind=kOutput, calls=%fused_computation.1 | convolution fusion | flops 681569280 | bytes 22958080 | tf_op jit(solution)/shard_map/fqhd,fkhd->fhqk/dot_general | solution.py:117
  86.5 4.6 %fusion = f32[10,512]{1,0:T(8,128)S(1)} fusion(f32[10,512,1024]{2,1,0:T(8,128)S(1)} %get-tuple-element.25, f32[10,512]{1,0:T(8,128)S(1)} %get-tuple-element.24), kind=kLoop, calls=%fused_computation.2 | loop fusion | flops 15723520 | bytes 21012480 | tf_op jit(solution)/shard_map/reduce_sum | solution.py:123
  91.1 3.0 %copy-done.2 = f32[10,512,1024]{2,1,0:T(8,128)} copy-done((f32[10,512,1024]{2,1,0:T(8,128)}, f32[10,512,1024]{2,1,0:T(8,128)S(1)}, u32[]{:S(2)}) %copy-start.2) | copy-done | bytes 20971544
  94.1 1.6 copy.52
  95.8 9.4 %divide_convert_fusion = bf16[10,512,64]{1,2,0:T(8,128)(2,1)S(1)} fusion(bf16[1024,10,64]{0,2,1:T(8,128)(2,1)S(1)} %bitcast.75, f32[10,512,1024]{2,1,0:T(8,128)} %copy-done.2, f32[10,512]{1,0:T(8,128)S(1)} %get-tuple-element.24, f32[10,512]{1,0:T(8,128)S(1)} %get-tuple-element.19, f32[10,512]{1,0:T(8,128)S(1)} %get-tuple-element.18), kind=kOutput, calls=%fused_computation.26 | convolution fusion | flops 687800320 | bytes 22999040 | tf_op jit(solution)/shard_map/fhqk,fkhd->fhqd/dot_general | solution.py:125
  106.6 2.1 %copy.73 = bf16[1,512,640]{2,0,1:T(2,128)(2,1)} copy(bf16[1,512,640]{2,1,0:T(8,128)(2,1)S(1)} %fusion.27) | data formatting | bytes 1310720 | tf_op jit(solution)/shard_map/convert_element_type | solution.py:36
  109.3 5.6 %reduce.17 = bf16[512,640]{1,0:T(8,128)(2,1)S(1)} reduce(bf16[512,1,640]{2,1,0:T(2,128)(2,1)} %bitcast.64, bf16[]{:T(256)} %broadcast.133), dimensions={1}, to_apply=%bitcast.61.reduce_sub_computation | reduce | bytes 1310722
  115.0 23.7 %all_to_all.8 = bf16[8,2,20480]{2,1,0:T(2,128)(2,1)S(1)} all-to-all(bf16[8,2,20480]{2,1,0:T(2,128)(2,1)S(1)} %reshape.213), channel_id=1, replica_groups=mesh['groups'=2,'frame'=8,'row'=2] {'frame'}, dimensions={0} | all-to-all | bytes 1310720 | tf_op jit(solution)/shard_map/all_to_all | solution.py:133
  139.4 3.4 %convolution_convert_fusion = bf16[512,1920]{1,0:T(8,128)(2,1)S(1)} fusion(bf16[640,1920]{1,0:T(8,128)(2,1)} %param.16, bf16[1,512,640]{2,0,1:T(2,128)(2,1)S(1)} %bitcast.76), kind=kOutput, calls=%fused_computation.6 | convolution fusion | flops 1259274240 | bytes 5079040 | tf_op jit(solution)/shard_map/dot_general | solution.py:42
  143.9 1.6 copy.66
  145.6 1.7 copy.57
  148.0 1.6 copy.58
  150.4 1.7 copy.59
  152.1 2.8 %multiply_reduce_fusion.1 = (f32[64,10,8]{2,1,0:T(8,128)S(1)}, f32[64,10,8,8]{2,3,1,0:T(8,128)S(1)}) fusion(bf16[8,64,10,64]{3,0,2,1:T(8,128)(2,1)} %copy.57, bf16[8,64,10,64]{3,0,2,1:T(8,128)(2,1)} %copy.58), kind=kOutput, calls=%fused_computation.12 | convolution fusion | flops 5319680 | bytes 1495040 | tf_op jit(solution)/shard_map/qphd,kphd->phqk/dot_general | solution.py:59
  156.3 2.5 %fusion.5 = bf16[8,64,10,64]{3,0,2,1:T(8,128)(2,1)} fusion(bf16[8,64,10,64]{3,0,2,1:T(8,128)(2,1)S(1)} %copy-done.8, f32[64,10,8,8]{2,3,1,0:T(8,128)S(1)} %get-tuple-element.29, f32[8,64,10]{0,2,1:T(8,128)S(1)} %bitcast.78, f32[64,10,8]{2,1,0:T(8,128)S(1)} %get-tuple-element.28), kind=kOutput, calls=%fused_computation.10 | convolution fusion | flops 6021120 | bytes 1515520 | tf_op jit(solution)/shard_map/phqk,kphd->qphd/dot_general | solution.py:65
  158.8 2.0 %copy.61 = bf16[8,64,10,64]{1,3,2,0:T(8,128)(2,1)S(1)} copy(bf16[8,64,10,64]{3,0,2,1:T(8,128)(2,1)} %fusion.5) | data formatting | bytes 1310720 | tf_op jit(solution)/shard_map/convert_element_type | solution.py:67
  161.4 20.6 %all_to_all.9 = bf16[8,64,640]{2,1,0:T(8,128)(2,1)S(1)} all-to-all(bf16[8,64,640]{2,1,0:T(8,128)(2,1)S(1)} %copy.62), channel_id=1, replica_groups=mesh['groups'=2,'frame'=8,'row'=2] {'frame'}, dimensions={0} | all-to-all | bytes 1310720 | tf_op jit(solution)/shard_map/all_to_all | solution.py:136
  182.0 3.3 %convolution_add_fusion = f32[512,640]{1,0:T(8,128)} fusion(f32[512,640]{1,0:T(8,128)} %copy-done.3, bf16[512,640]{1,0:T(8,128)(2,1)S(1)} %bitcast.70, bf16[640,640]{1,0:T(8,128)(2,1)S(1)} %copy-done.10), kind=kOutput, calls=%fused_computation.16 | convolution fusion | flops 419758080 | bytes 4096000 | tf_op jit(solution)/shard_map/dot_general | solution.py:72
  (67 shorter events, 17.5 us)
Async XLA Ops:
  6.5 65.3 %copy-start = (bf16[640,1920]{1,0:T(8,128)(2,1)S(1)}, bf16[640,1920]{1,0:T(8,128)(2,1)}, u32[]{:S(2)}) copy-start(bf16[640,1920]{1,0:T(8,128)(2,1)} %param.13) | copy-start | bytes 7372804
  6.5 75.3 %all-gather.3.cloned.1.call-start = ((), (), s32[]{:S(2)}) async-start(), calls=%async_computation.2 | async-start | bytes 1966080 | tf_op jit(solution)/shard_map/all_gather | solution.py:112
  6.5 58.0 %collective-permute-start = (bf16[1,8,64,640]{3,2,1,0:T(8,128)(2,1)}, bf16[1,8,64,640]{3,2,1,0:T(8,128)(2,1)S(1)}, u32[]{:S(2)}, u32[]{:S(2)}) collective-permute-start(bf16[1,8,64,640]{3,2,1,0:T(8,128)(2,1)} %param.9), channel_id=1, source_target_pairs={{0,2},{2,4},{4,6},{6,8},{8,10},{10,12},{12,14},{1,3},{3,5},{5,7},{... | collective-permute-start | bytes 1966088 | tf_op jit(solution)/shard_map/ppermute | solution.py:16
  11.6 52.9 %collective-permute-start.1 = (bf16[1,8,64,640]{3,2,1,0:T(8,128)(2,1)}, bf16[1,8,64,640]{3,2,1,0:T(8,128)(2,1)}, u32[]{:S(2)}, u32[]{:S(2)}) collective-permute-start(bf16[1,8,64,640]{3,2,1,0:T(8,128)(2,1)} %param.9), channel_id=1, source_target_pairs={{2,0},{4,2},{6,4},{8,6},{10,8},{12,10},{14,12},{3,1},{5,3},{7,5},{... | collective-permute-start | bytes 1966088 | tf_op jit(solution)/shard_map/ppermute | solution.py:19
  67.0 1.7 copy-start.7
  69.5 1.1 copy-start.6
  70.6 1.3 copy-start.12
  71.5 2.2 %copy-start.4 = (f32[512,640]{1,0:T(8,128)}, f32[512,640]{1,0:T(8,128)S(1)}, u32[]{:S(2)}) copy-start(f32[512,640]{1,0:T(8,128)S(1)} %get-tuple-element.23) | copy-start | bytes 3932164
  75.0 19.1 %all-gather.5.cloned.1.call-start = ((), (), s32[]{:S(2)}) async-start(), calls=%async_computation.3 | async-start | bytes 1966080 | tf_op jit(solution)/shard_map/all_gather | solution.py:113
  86.5 7.6 %copy-start.2 = (f32[10,512,1024]{2,1,0:T(8,128)}, f32[10,512,1024]{2,1,0:T(8,128)S(1)}, u32[]{:S(2)}) copy-start(f32[10,512,1024]{2,1,0:T(8,128)S(1)} %get-tuple-element.25) | copy-start | bytes 62914564
  95.7 9.4 %copy-start.5 = (f32[512,640]{1,0:T(8,128)S(1)}, f32[512,640]{1,0:T(8,128)}, u32[]{:S(2)}) copy-start(f32[512,640]{1,0:T(8,128)} %copy-done.4) | copy-start | bytes 3932164
  95.8 9.4 %copy-start.9 = (bf16[640,640]{1,0:T(8,128)(2,1)S(1)}, bf16[640,640]{1,0:T(8,128)(2,1)}, u32[]{:S(2)}) copy-start(bf16[640,640]{1,0:T(8,128)(2,1)} %param.14) | copy-start | bytes 2457604
  105.2 1.2 copy-start.11
  106.1 2.6 %copy-start.3 = (f32[512,640]{1,0:T(8,128)}, f32[512,640]{1,0:T(8,128)S(1)}, u32[]{:S(2)}) copy-start(f32[512,640]{1,0:T(8,128)S(1)} %get-tuple-element.27) | copy-start | bytes 3932164
  154.9 1.3 copy-start.8
  160.8 21.2 %copy-start.10 = (bf16[640,640]{1,0:T(8,128)(2,1)S(1)}, bf16[640,640]{1,0:T(8,128)(2,1)}, u32[]{:S(2)}) copy-start(bf16[640,640]{1,0:T(8,128)(2,1)} %param.17) | copy-start | bytes 2457604
  182.0 3.3 %copy-start.1 = (bf16[640,1920]{1,0:T(8,128)(2,1)S(1)}, bf16[640,1920]{1,0:T(8,128)(2,1)}, u32[]{:S(2)}) copy-start(bf16[640,1920]{1,0:T(8,128)(2,1)} %param.13) | copy-start | bytes 7372804
Sparse Core Ops, SparseCore 0:
  75.1 6.6 all-gather.2
  83.4 10.5 all-gather.4
where the time goes:
time: 193 us; the launch traced here: 192 us
  blocking collectives  93.8 us (49%)
  matrix products  29.7 us (15%)
  local copies, waits for them, and re-layouts  25.7 us (13%)
  other arithmetic  16.2 us (8%)
  between operations  13.8 us (7%)
  starting transfers between devices  6.55 us (3%)
  waiting for transfers between devices  6.39 us (3%)
    psum x1, blocking collectives, body(): first, second = lax.psum((first, second), ('frame', 'row'))  49.5 us
    all_to_all x1, blocking collectives, body(): lax.all_to_all(normed, 'frame', split_axis=1, concat_axis=0, tiled=True)  23.7 us
    all_to_all x1, blocking collectives, body(): lax.all_to_all(result, 'frame', split_axis=0, concat_axis=1, tiled=True)  20.6 us
    unnamed x32, local copies, waits for them, and re-layouts  9.47 us
    dot_general x1, matrix products, body(): jnp.einsum('fhqk,fkhd->fhqd', weights, value_heads, preferred_element_typ...  9.35 us
    all_gather x1, waiting for transfers between devices, body(): key_piece = lax.all_gather(key_rows, 'row', axis=1, tiled=True)  6.1 us
    unnamed x1, other arithmetic  5.57 us
    dot_general x2, matrix products, project_three(): jnp.dot(inputs.reshape(-1, channels), weight, preferred_element_type=jnp....  5.31 us
  transfers between devices with their start and end apart: 4, of which 1 were waited for; matrix products, arithmetic and copies ran while one was open for 6% of the time, Pallas kernels for 0%

commit v1 on v0

--- a/solution.py
+++ b/solution.py
@@ -85,7 +85,7 @@
     grouped = latent.astype(jnp.float32).reshape(frames, row_count, col_count, GROUPS, per_group)
     first = jnp.sum(grouped, axis=(0, 1, 2, 4))
     second = jnp.sum(grouped * grouped, axis=(0, 1, 2, 4))
-    first, second = lax.psum((first, second), ("frame", "row"))
+    first, second = lax.psum(lax.psum((first, second), "frame"), "row")
     number = frames * lax.axis_size("frame") * pixels * lax.axis_size("row") * per_group
     wide = padded_2(latent, (("frame", 0),), 1)
     wide_frames = wide.shape[0]

time: 193 us -> 185 us (0.959)
  blocking collectives: 93.8 us -> 84.3 us
  waiting for transfers between devices: 6.39 us -> 8.38 us
    psum x1 -> x2, blocking collectives: 49.5 us -> 40 us  [body(): first, second = lax.psum(lax.psum((first, second), 'frame'), 'row')]
    all_gather x1, waiting for transfers between devices: 6.1 us -> 8.09 us  [body(): key_piece = lax.all_gather(key_rows, 'row', axis=1, tiled=True)]
where the time goes in v1:
time: 185 us
  blocking collectives  84.3 us (46%)
  matrix products  29.6 us (16%)
  local copies, waits for them, and re-layouts  25.7 us (14%)
  other arithmetic  16.2 us (9%)
  between operations  13.8 us (7%)
  waiting for transfers between devices  8.38 us (5%)
  starting transfers between devices  6.55 us (4%)
    psum x2, blocking collectives, body(): first, second = lax.psum(lax.psum((first, second), 'frame'), 'row')  40 us
    all_to_all x1, blocking collectives, body(): lax.all_to_all(normed, 'frame', split_axis=1, concat_axis=0, tiled=True)  23.7 us
    all_to_all x1, blocking collectives, body(): lax.all_to_all(result, 'frame', split_axis=0, concat_axis=1, tiled=True)  20.6 us
    unnamed x32, local copies, waits for them, and re-layouts  9.47 us
    dot_general x1, matrix products, body(): jnp.einsum('fhqk,fkhd->fhqd', weights, value_heads, preferred_element_typ...  9.36 us
    all_gather x1, waiting for transfers between devices, body(): key_piece = lax.all_gather(key_rows, 'row', axis=1, tiled=True)  8.09 us
    unnamed x1, other arithmetic  5.57 us
    dot_general x2, matrix products, project_three(): jnp.dot(inputs.reshape(-1, channels), weight, preferred_element_type=jnp....  5.31 us
  transfers between devices with their start and end apart: 4, of which 1 were waited for; matrix products, arithmetic and copies ran while one was open for 6% of the time, Pallas kernels for 0%

profile of v1, /device:TPU:0, one launch (start us, length us, event | category | flops | bytes accessed | tf_op | source)
XLA Modules:
  0.0 184.6 jit_solution(1054789952144548824)
XLA Ops:
  6.5 5.0 %collective-permute-start = (bf16[1,8,64,640]{3,2,1,0:T(8,128)(2,1)}, bf16[1,8,64,640]{3,2,1,0:T(8,128)(2,1)S(1)}, u32[]{:S(2)}, u32[]{:S(2)}) collective-permute-start(bf16[1,8,64,640]{3,2,1,0:T(8,128)(2,1)} %param.9), channel_id=1, source_target_pairs={{0,2},{2,4},{4,6},{6,8},{8,10},{10,12},{12,14},{1,3},{3,5},{5,7},{... | collective-permute-start | bytes 1966088 | tf_op jit(solution)/shard_map/ppermute | solution.py:16
  14.6 37.6 %all-reduce = (f32[32]{0:T(128)S(1)}, f32[32]{0:T(128)S(1)}) all-reduce(f32[32]{0:T(128)S(1)} %reduce_sum.91, f32[32]{0:T(128)S(1)} %reduce_sum.88), channel_id=1, replica_groups=mesh['groups'=2,'frame'=8,'row'=2] {'frame'}, use_global_device_ids=true, to_apply=%region_6.7 | all-reduce | flops 64 | bytes 512 | tf_op jit(solution)/shard_map/psum | solution.py:88
  52.2 2.5 %all-reduce.1 = (f32[32]{0:T(128)S(1)}, f32[32]{0:T(128)S(1)}) all-reduce(f32[32]{0:T(128)S(1)} %get-tuple-element.7, f32[32]{0:T(128)S(1)} %get-tuple-element.8), channel_id=1, replica_groups=mesh['groups'=2,'frame'=8,'row'=2] {'row'}, use_global_device_ids=true, to_apply=%region_7.8 | all-reduce | flops 64 | bytes 512 | tf_op jit(solution)/shard_map/psum | solution.py:88
  55.0 2.5 %fusion.8 = bf16[3,8,64,640]{3,2,1,0:T(8,128)(2,1)S(1)} fusion(bf16[1,8,64,640]{3,2,1,0:T(8,128)(2,1)} %collective-permute-done.1, bf16[1,8,64,640]{3,2,1,0:T(8,128)(2,1)} %param.9, bf16[1,8,64,640]{3,2,1,0:T(8,128)(2,1)S(1)} %collective-permute-done, f32[640]{0:T(1024)} %param.10, f32[640]{0:T(1024)S(1)} %mul.99, f32[640]{0:T(1024)S(1)} %sub.69, ...), kind=kLoop, calls=%fused_computation.15 | loop fusion | flops 11796480 | bytes 3939843 | tf_op jit(solution)/shard_map/jit(_where)/select_n | solution.py:99
  62.4 1.9 %fusion.4 = bf16[1,512,1920]{2,1,0:T(8,128)(2,1)S(1)} fusion(bf16[640,1920]{1,0:T(8,128)(2,1)S(1)} %copy-done, f32[512,640]{1,0:T(8,128)S(1)} %get-tuple-element.25, f32[640]{0:T(1024)S(1)} %copy-done.12, f32[512]{0:T(512)S(1)} %add_rsqrt_fusion.1, f32[512]{0:T(512)S(1)} %broadcast_multiply_fusion.1), kind=kOutput, calls=%fused_computation.8 | convolution fusion | flops 1260584960 | bytes 5741056 | tf_op jit(solution)/shard_map/dot_general | solution.py:42
  66.3 8.1 %all-gather.3.cloned.1.call-done = bf16[1,1024,640]{2,1,0:T(8,128)(2,1)} async-done(((bf16[1,512,640]{2,1,0:T(8,128)(2,1)}), bf16[1,1024,640]{2,1,0:T(8,128)(2,1)}) %all-gather.3.cloned.1.call-update) | async-done | bytes 1310736 | tf_op jit(solution)/shard_map/all_gather | solution.py:112
  76.0 3.0 %multiply_reduce_fusion = (f32[10,512]{1,0:T(8,128)S(1)}, f32[10,512,1024]{2,1,0:T(8,128)S(1)}) fusion(bf16[512,10,64]{0,2,1:T(8,128)(2,1)S(1)} %bitcast.69, bf16[1024,10,64]{0,2,1:T(8,128)(2,1)S(1)} %bitcast.63), kind=kOutput, calls=%fused_computation.1 | convolution fusion | flops 681569280 | bytes 22958080 | tf_op jit(solution)/shard_map/fqhd,fkhd->fhqk/dot_general | solution.py:117
  79.0 4.6 %fusion = f32[10,512]{1,0:T(8,128)S(1)} fusion(f32[10,512,1024]{2,1,0:T(8,128)S(1)} %get-tuple-element.27, f32[10,512]{1,0:T(8,128)S(1)} %get-tuple-element.26), kind=kLoop, calls=%fused_computation.2 | loop fusion | flops 15723520 | bytes 21012480 | tf_op jit(solution)/shard_map/reduce_sum | solution.py:123
  83.6 3.0 %copy-done.2 = f32[10,512,1024]{2,1,0:T(8,128)} copy-done((f32[10,512,1024]{2,1,0:T(8,128)}, f32[10,512,1024]{2,1,0:T(8,128)S(1)}, u32[]{:S(2)}) %copy-start.2) | copy-done | bytes 20971544
  86.6 1.6 copy.52
  88.3 9.4 %divide_convert_fusion = bf16[10,512,64]{1,2,0:T(8,128)(2,1)S(1)} fusion(bf16[1024,10,64]{0,2,1:T(8,128)(2,1)S(1)} %bitcast.75, f32[10,512,1024]{2,1,0:T(8,128)} %copy-done.2, f32[10,512]{1,0:T(8,128)S(1)} %get-tuple-element.26, f32[10,512]{1,0:T(8,128)S(1)} %get-tuple-element.21, f32[10,512]{1,0:T(8,128)S(1)} %get-tuple-element.20), kind=kOutput, calls=%fused_computation.26 | convolution fusion | flops 687800320 | bytes 22999040 | tf_op jit(solution)/shard_map/fhqk,fkhd->fhqd/dot_general | solution.py:125
  99.1 2.1 %copy.73 = bf16[1,512,640]{2,0,1:T(2,128)(2,1)} copy(bf16[1,512,640]{2,1,0:T(8,128)(2,1)S(1)} %fusion.27) | data formatting | bytes 1310720 | tf_op jit(solution)/shard_map/convert_element_type | solution.py:36
  101.7 5.6 %reduce.17 = bf16[512,640]{1,0:T(8,128)(2,1)S(1)} reduce(bf16[512,1,640]{2,1,0:T(2,128)(2,1)} %bitcast.64, bf16[]{:T(256)} %broadcast.133), dimensions={1}, to_apply=%bitcast.61.reduce_sub_computation | reduce | bytes 1310722
  107.5 23.7 %all_to_all.8 = bf16[8,2,20480]{2,1,0:T(2,128)(2,1)S(1)} all-to-all(bf16[8,2,20480]{2,1,0:T(2,128)(2,1)S(1)} %reshape.213), channel_id=1, replica_groups=mesh['groups'=2,'frame'=8,'row'=2] {'frame'}, dimensions={0} | all-to-all | bytes 1310720 | tf_op jit(solution)/shard_map/all_to_all | solution.py:133
  131.8 3.4 %convolution_convert_fusion = bf16[512,1920]{1,0:T(8,128)(2,1)S(1)} fusion(bf16[640,1920]{1,0:T(8,128)(2,1)} %param.16, bf16[1,512,640]{2,0,1:T(2,128)(2,1)S(1)} %bitcast.76), kind=kOutput, calls=%fused_computation.6 | convolution fusion | flops 1259274240 | bytes 5079040 | tf_op jit(solution)/shard_map/dot_general | solution.py:42
  136.4 1.6 copy.66
  138.1 1.7 copy.57
  140.5 1.6 copy.58
  142.9 1.7 copy.59
  144.6 2.8 %multiply_reduce_fusion.1 = (f32[64,10,8]{2,1,0:T(8,128)S(1)}, f32[64,10,8,8]{2,3,1,0:T(8,128)S(1)}) fusion(bf16[8,64,10,64]{3,0,2,1:T(8,128)(2,1)} %copy.57, bf16[8,64,10,64]{3,0,2,1:T(8,128)(2,1)} %copy.58), kind=kOutput, calls=%fused_computation.12 | convolution fusion | flops 5319680 | bytes 1495040 | tf_op jit(solution)/shard_map/qphd,kphd->phqk/dot_general | solution.py:59
  148.7 2.5 %fusion.5 = bf16[8,64,10,64]{3,0,2,1:T(8,128)(2,1)} fusion(bf16[8,64,10,64]{3,0,2,1:T(8,128)(2,1)S(1)} %copy-done.8, f32[64,10,8,8]{2,3,1,0:T(8,128)S(1)} %get-tuple-element.31, f32[8,64,10]{0,2,1:T(8,128)S(1)} %bitcast.78, f32[64,10,8]{2,1,0:T(8,128)S(1)} %get-tuple-element.30), kind=kOutput, calls=%fused_computation.10 | convolution fusion | flops 6021120 | bytes 1515520 | tf_op jit(solution)/shard_map/phqk,kphd->qphd/dot_general | solution.py:65
  151.3 2.0 %copy.61 = bf16[8,64,10,64]{1,3,2,0:T(8,128)(2,1)S(1)} copy(bf16[8,64,10,64]{3,0,2,1:T(8,128)(2,1)} %fusion.5) | data formatting | bytes 1310720 | tf_op jit(solution)/shard_map/convert_element_type | solution.py:67
  153.9 20.6 %all_to_all.9 = bf16[8,64,640]{2,1,0:T(8,128)(2,1)S(1)} all-to-all(bf16[8,64,640]{2,1,0:T(8,128)(2,1)S(1)} %copy.62), channel_id=1, replica_groups=mesh['groups'=2,'frame'=8,'row'=2] {'frame'}, dimensions={0} | all-to-all | bytes 1310720 | tf_op jit(solution)/shard_map/all_to_all | solution.py:136
  174.5 3.3 %convolution_add_fusion = f32[512,640]{1,0:T(8,128)} fusion(f32[512,640]{1,0:T(8,128)} %copy-done.3, bf16[512,640]{1,0:T(8,128)(2,1)S(1)} %bitcast.70, bf16[640,640]{1,0:T(8,128)(2,1)S(1)} %copy-done.10), kind=kOutput, calls=%fused_computation.16 | convolution fusion | flops 419758080 | bytes 4096000 | tf_op jit(solution)/shard_map/dot_general | solution.py:72
  (68 shorter events, 19.1 us)
Async XLA Ops:
  6.5 55.8 %copy-start = (bf16[640,1920]{1,0:T(8,128)(2,1)S(1)}, bf16[640,1920]{1,0:T(8,128)(2,1)}, u32[]{:S(2)}) copy-start(bf16[640,1920]{1,0:T(8,128)(2,1)} %param.13) | copy-start | bytes 7372804
  6.5 67.8 %all-gather.3.cloned.1.call-start = ((), (), s32[]{:S(2)}) async-start(), calls=%async_computation.2 | async-start | bytes 1966080 | tf_op jit(solution)/shard_map/all_gather | solution.py:112
  6.5 48.5 %collective-permute-start = (bf16[1,8,64,640]{3,2,1,0:T(8,128)(2,1)}, bf16[1,8,64,640]{3,2,1,0:T(8,128)(2,1)S(1)}, u32[]{:S(2)}, u32[]{:S(2)}) collective-permute-start(bf16[1,8,64,640]{3,2,1,0:T(8,128)(2,1)} %param.9), channel_id=1, source_target_pairs={{0,2},{2,4},{4,6},{6,8},{8,10},{10,12},{12,14},{1,3},{3,5},{5,7},{... | collective-permute-start | bytes 1966088 | tf_op jit(solution)/shard_map/ppermute | solution.py:16
  11.6 43.4 %collective-permute-start.1 = (bf16[1,8,64,640]{3,2,1,0:T(8,128)(2,1)}, bf16[1,8,64,640]{3,2,1,0:T(8,128)(2,1)}, u32[]{:S(2)}, u32[]{:S(2)}) collective-permute-start(bf16[1,8,64,640]{3,2,1,0:T(8,128)(2,1)} %param.9), channel_id=1, source_target_pairs={{2,0},{4,2},{6,4},{8,6},{10,8},{12,10},{14,12},{3,1},{5,3},{7,5},{... | collective-permute-start | bytes 1966088 | tf_op jit(solution)/shard_map/ppermute | solution.py:19
  57.5 1.7 copy-start.7
  60.0 1.1 copy-start.6
  61.1 1.3 copy-start.12
  62.0 2.2 %copy-start.4 = (f32[512,640]{1,0:T(8,128)}, f32[512,640]{1,0:T(8,128)S(1)}, u32[]{:S(2)}) copy-start(f32[512,640]{1,0:T(8,128)S(1)} %get-tuple-element.25) | copy-start | bytes 3932164
  65.5 21.1 %all-gather.5.cloned.1.call-start = ((), (), s32[]{:S(2)}) async-start(), calls=%async_computation.3 | async-start | bytes 1966080 | tf_op jit(solution)/shard_map/all_gather | solution.py:113
  79.0 7.6 %copy-start.2 = (f32[10,512,1024]{2,1,0:T(8,128)}, f32[10,512,1024]{2,1,0:T(8,128)S(1)}, u32[]{:S(2)}) copy-start(f32[10,512,1024]{2,1,0:T(8,128)S(1)} %get-tuple-element.27) | copy-start | bytes 62914564
  88.2 9.4 %copy-start.5 = (f32[512,640]{1,0:T(8,128)S(1)}, f32[512,640]{1,0:T(8,128)}, u32[]{:S(2)}) copy-start(f32[512,640]{1,0:T(8,128)} %copy-done.4) | copy-start | bytes 3932164
  88.2 9.4 %copy-start.9 = (bf16[640,640]{1,0:T(8,128)(2,1)S(1)}, bf16[640,640]{1,0:T(8,128)(2,1)}, u32[]{:S(2)}) copy-start(bf16[640,640]{1,0:T(8,128)(2,1)} %param.14) | copy-start | bytes 2457604
  97.6 1.2 copy-start.11
  98.6 2.6 %copy-start.3 = (f32[512,640]{1,0:T(8,128)}, f32[512,640]{1,0:T(8,128)S(1)}, u32[]{:S(2)}) copy-start(f32[512,640]{1,0:T(8,128)S(1)} %get-tuple-element.29) | copy-start | bytes 3932164
  147.4 1.3 copy-start.8
  153.3 21.2 %copy-start.10 = (bf16[640,640]{1,0:T(8,128)(2,1)S(1)}, bf16[640,640]{1,0:T(8,128)(2,1)}, u32[]{:S(2)}) copy-start(bf16[640,640]{1,0:T(8,128)(2,1)} %param.17) | copy-start | bytes 2457604
  174.5 3.3 %copy-start.1 = (bf16[640,1920]{1,0:T(8,128)(2,1)S(1)}, bf16[640,1920]{1,0:T(8,128)(2,1)}, u32[]{:S(2)}) copy-start(bf16[640,1920]{1,0:T(8,128)(2,1)} %param.13) | copy-start | bytes 7372804
Sparse Core Ops, SparseCore 0:
  65.6 8.6 all-gather.2
  75.9 10.5 all-gather.4
